TPU v7x, 32 devices: a whole 2x2x4 slice. The times are simulated.
32 devices in a mesh: dp: 8 (over z, y), tensor: 4 (over x, core).
Axes of the slice: x: 2, y: 2, z: 4, core: 2. Of those that a mesh axis runs over, the one named last changes fastest.
Arguments:
- tokens: bfloat16 [16384, 768], P(('dp', 'tensor')), may hold values from -6 to 6
- grad_out: bfloat16 [16384, 768], P(('dp', 'tensor')), may hold values from -6 to 6
- seg_ids: int32 [16, 1024], P('dp'), may hold values from 0 to 5, never falling along the last dimension, each value on 1 to 800 neighbouring positions
- w_qkv: bfloat16 [3, 768, 768], P(None, 'dp', 'tensor'), may hold values from -0.21875 to 0.21875
- b_qv: bfloat16 [2, 768], P(None, ('tensor', 'dp')), may hold values from -3 to 3
- w_out: bfloat16 [768, 768], P('tensor', 'dp'), may hold values from -1.75 to 1.75
- w_up: bfloat16 [768, 3072], P('dp', 'tensor'), may hold values from -0.21875 to 0.21875
- b_up: bfloat16 [3072], P(('tensor', 'dp')), may hold values from -3 to 3
- w_down: bfloat16 [3072, 768], P('tensor', 'dp'), may hold values from -0.21875 to 0.21875
- b_out: float32 [768], P(('dp', 'tensor')), may hold values from -2 to 2
- b_down: float32 [768], P(('dp', 'tensor')), may hold values from -2 to 2
- g_one: float32 [768], P(('dp', 'tensor')), may hold values from 0.5 to 1.5
- s_one: float32 [768], P(('dp', 'tensor')), may hold values from -2 to 2
- g_two: float32 [768], P(('dp', 'tensor')), may hold values from 0.5 to 1.5
- s_two: float32 [768], P(('dp', 'tensor')), may hold values from -2 to 2
Outputs:
- layer_out: bfloat16 [16384, 768], P(('dp', 'tensor'))
- input_grad: bfloat16 [16384, 768], P(('dp', 'tensor'))
- grad_qkv: float32 [3, 768, 768], P(None, 'dp', 'tensor')
- grad_bias_qv: float32 [2, 768], P(None, ('tensor', 'dp'))
- grad_out_proj: float32 [768, 768], P('tensor', 'dp')
- grad_up: float32 [768, 3072], P('dp', 'tensor')
- grad_bias_up: float32 [3072], P(('tensor', 'dp'))
- grad_down: float32 [3072, 768], P('tensor', 'dp')
- grad_bias_out: float32 [768], P(('dp', 'tensor'))
- grad_bias_down: float32 [768], P(('dp', 'tensor'))
- grad_gain_one: float32 [768], P(('dp', 'tensor'))
- grad_shift_one: float32 [768], P(('dp', 'tensor'))
- grad_gain_two: float32 [768], P(('dp', 'tensor'))
- grad_shift_two: float32 [768], P(('dp', 'tensor'))
Inputs may be any that keep to these rules, and one draw needn't show every extreme that they name: `seg_ids`: within a sequence the ids never fall; each document spans 1 to 800 tokens, and the longest one of a draw spans exactly 800.
All inputs are finite; a program needn't handle non-finite values.
Results may differ from a plain program's by a relative error of at most 0.024.
Values may be sent and summed in bfloat16 or wider, within the bound.
No kernel may reach another device: no remote copies, remote signals or barrier semaphores. Data moves between devices by JAX's collectives and lax.ppermute only.
A program may use at most 128 MiB of HBM per device.

v0:
```python
import jax
import jax.numpy as jnp
from jax import lax
from jax.sharding import PartitionSpec as P

HD = 64
EPSILON = 1e-05
ROOT_HALF = 0.7071067811865476


def norm_rows(r, gain, shift):
    mean = jnp.mean(r, axis=-1, keepdims=True)
    cent = r - mean
    var = jnp.mean(cent * cent, axis=-1, keepdims=True)
    return cent * lax.rsqrt(var + EPSILON) * gain + shift


def gelu_exact(u):
    return 0.5 * u * (1.0 + lax.erf(u * ROOT_HALF))


def masked_scores(query, keys, seg_query, seg_keys):
    raw = jnp.einsum("qhd,khd->hqk", query, keys, preferred_element_type=jnp.float32)
    same = seg_query[:, None] == seg_keys[None, :]
    return jnp.where(same[None], raw * 0.125, -1000000000.0)


def attend_forward(query, keys, values, seg_query, seg_keys):
    scores = masked_scores(query, keys, seg_query, seg_keys)
    top = jnp.max(scores, axis=-1, keepdims=True)
    expo = jnp.exp(scores - top)
    total = jnp.sum(expo, axis=-1, keepdims=True)
    probs = (expo / total).astype(jnp.bfloat16)
    context = jnp.einsum("hqk,khd->qhd", probs, values, preferred_element_type=jnp.float32)
    return (context.astype(jnp.bfloat16), top + jnp.log(total))


def attend_backward(query, keys, values, seg_query, seg_keys, lse_block, d_block):
    scores = masked_scores(query, keys, seg_query, seg_keys)
    probs = jnp.exp(scores - lse_block)
    probs_low = probs.astype(jnp.bfloat16)
    d_probs = jnp.einsum("qhd,khd->hqk", d_block, values, preferred_element_type=jnp.float32)
    inner = jnp.sum(probs * d_probs, axis=-1, keepdims=True)
    d_scores = (probs * (d_probs - inner)).astype(jnp.bfloat16)
    d_query = jnp.einsum("hqk,khd->qhd", d_scores, keys, preferred_element_type=jnp.float32) * 0.125
    d_keys = jnp.einsum("hqk,qhd->khd", d_scores, query, preferred_element_type=jnp.float32) * 0.125
    d_values = jnp.einsum("hqk,qhd->khd", probs_low, d_block, preferred_element_type=jnp.float32)
    return (d_query, d_keys, d_values)


def contract_rows(left, right):
    return lax.dot_general(
        left, right, (((0,), (0,)), ((), ())), preferred_element_type=jnp.float32
    )


def contract_cols(left, right):
    return lax.dot_general(
        left, right, (((1,), (1,)), ((), ())), preferred_element_type=jnp.float32
    )


def local(
    tokens,
    grad_out,
    seg_ids,
    w_qkv,
    b_qv,
    w_out,
    w_up,
    b_up,
    w_down,
    b_out,
    b_down,
    g_one,
    s_one,
    g_two,
    s_two,
):
    seqs, seq_len = seg_ids.shape
    group = seqs * seq_len
    block = min(512, seq_len)
    nblocks = seq_len // block
    items = seqs * nblocks
    wqkv_l, bqv_l, wout_l, wup_l, bup_l, wdown_l = (
        lax.all_gather(w_qkv, "dp", axis=1, tiled=True),
        lax.all_gather(b_qv, "dp", axis=1, tiled=True),
        lax.all_gather(w_out, "dp", axis=1, tiled=True),
        lax.all_gather(w_up, "dp", axis=0, tiled=True),
        lax.all_gather(b_up, "dp", axis=0, tiled=True),
        lax.all_gather(w_down, "dp", axis=1, tiled=True),
    )
    bout_f, bdown_f, gone_f, sone_f, gtwo_f, stwo_f = (
        lax.all_gather(b_out, ("dp", "tensor"), axis=0, tiled=True),
        lax.all_gather(b_down, ("dp", "tensor"), axis=0, tiled=True),
        lax.all_gather(g_one, ("dp", "tensor"), axis=0, tiled=True),
        lax.all_gather(s_one, ("dp", "tensor"), axis=0, tiled=True),
        lax.all_gather(g_two, ("dp", "tensor"), axis=0, tiled=True),
        lax.all_gather(s_two, ("dp", "tensor"), axis=0, tiled=True),
    )
    local_width = wqkv_l.shape[2]
    local_heads = local_width // HD
    x_full = lax.all_gather(tokens, "tensor", axis=0, tiled=True)
    proj = jnp.einsum("td,jde->jte", x_full, wqkv_l, preferred_element_type=jnp.float32)
    biases = jnp.stack([bqv_l[0], jnp.zeros_like(bqv_l[0]), bqv_l[1]]).astype(jnp.float32)
    proj = (proj + biases[:, None, :]).astype(jnp.bfloat16)
    heads = proj.reshape(3, seqs, seq_len, local_heads, HD)
    queries = heads[0].reshape(items, block, local_heads, HD)
    seg_blocks = seg_ids.reshape(items, block)
    owner = jnp.arange(items, dtype=jnp.int32) // nblocks

    def forward_item(item):
        query, seg_query, which = item
        return attend_forward(query, heads[1][which], heads[2][which], seg_query, seg_ids[which])

    context, lse = lax.map(forward_item, (queries, seg_blocks, owner))
    context = context.reshape(group, local_width)
    part = context
    attn = (
        lax.psum_scatter(
            jnp.dot(part, wout_l, preferred_element_type=jnp.float32).astype(jnp.bfloat16),
            "tensor",
            scatter_dimension=0,
            tiled=True,
        ).astype(jnp.float32)
        + bout_f
    )
    first = tokens.astype(jnp.float32) + attn
    normed = norm_rows(first, gone_f, sone_f)
    normed_full = lax.all_gather(normed.astype(jnp.bfloat16), "tensor", axis=0, tiled=True)
    up = jnp.dot(normed_full, wup_l, preferred_element_type=jnp.float32) + bup_l.astype(jnp.float32)
    hidden = gelu_exact(up).astype(jnp.bfloat16)
    part = hidden
    branch = (
        lax.psum_scatter(
            jnp.dot(part, wdown_l, preferred_element_type=jnp.float32).astype(jnp.bfloat16),
            "tensor",
            scatter_dimension=0,
            tiled=True,
        ).astype(jnp.float32)
        + bdown_f
    )
    second = normed + branch
    layer_out = norm_rows(second, gtwo_f, stwo_f)
    wqkv_b, wout_b, wup_b, wdown_b = (
        lax.all_gather(w_qkv, "dp", axis=1, tiled=True),
        lax.all_gather(w_out, "dp", axis=1, tiled=True),
        lax.all_gather(w_up, "dp", axis=0, tiled=True),
        lax.all_gather(w_down, "dp", axis=1, tiled=True),
    )
    _, pull_two = jax.vjp(norm_rows, second, gtwo_f, stwo_f)
    d_second, d_gain_two, d_shift_two = pull_two(grad_out.astype(jnp.float32))
    d_branch = d_second.astype(jnp.bfloat16)
    d_bias_down = jnp.sum(d_branch.astype(jnp.float32), axis=0)
    branch_full = lax.all_gather(d_branch, "tensor", axis=0, tiled=True)
    grad_down_w = contract_rows(hidden, branch_full)
    d_hidden = contract_cols(branch_full, wdown_b)
    _, pull_gelu = jax.vjp(gelu_exact, up)
    d_up = pull_gelu(d_hidden)[0].astype(jnp.bfloat16)
    grad_bias_up = jnp.sum(d_up.astype(jnp.float32), axis=0)
    grad_up_w = contract_rows(normed_full, d_up)
    part = d_up
    d_normed = d_second + lax.psum_scatter(
        contract_cols(part, wup_b).astype(jnp.bfloat16), "tensor", scatter_dimension=0, tiled=True
    ).astype(jnp.float32)
    _, pull_one = jax.vjp(norm_rows, first, gone_f, sone_f)
    d_first, d_gain_one, d_shift_one = pull_one(d_normed)
    d_attn = d_first.astype(jnp.bfloat16)
    d_bias_out = jnp.sum(d_attn.astype(jnp.float32), axis=0)
    attn_full = lax.all_gather(d_attn, "tensor", axis=0, tiled=True)
    grad_out_w = contract_rows(context, attn_full)
    d_context = contract_cols(attn_full, wout_b).astype(jnp.bfloat16)
    d_ctx_blocks = d_context.reshape(items, block, local_heads, HD)

    def backward_item(item):
        query, seg_query, which, lse_block, d_block = item
        return attend_backward(
            query, heads[1][which], heads[2][which], seg_query, seg_ids[which], lse_block, d_block
        )

    d_query, d_keys, d_values = lax.map(
        backward_item, (queries, seg_blocks, owner, lse, d_ctx_blocks)
    )
    d_keys = jnp.sum(d_keys.reshape(seqs, nblocks, seq_len, local_heads, HD), axis=1)
    d_values = jnp.sum(d_values.reshape(seqs, nblocks, seq_len, local_heads, HD), axis=1)
    d_proj = jnp.stack(
        [
            d_query.reshape(group, local_width),
            d_keys.reshape(group, local_width),
            d_values.reshape(group, local_width),
        ]
    ).astype(jnp.bfloat16)
    proj_sums = jnp.sum(d_proj.astype(jnp.float32), axis=1)
    grad_bias_qv = jnp.stack([proj_sums[0], proj_sums[2]])
    grad_qkv_w = jnp.einsum("td,jte->jde", x_full, d_proj, preferred_element_type=jnp.float32)
    part = d_proj
    d_tokens = d_first + lax.psum_scatter(
        jnp.einsum("jte,jde->td", part, wqkv_b, preferred_element_type=jnp.float32).astype(
            jnp.bfloat16
        ),
        "tensor",
        scatter_dimension=0,
        tiled=True,
    ).astype(jnp.float32)
    g_qkv, g_bqv, g_out, g_up, g_bup, g_down = (
        lax.psum_scatter(grad_qkv_w, "dp", scatter_dimension=1, tiled=True),
        lax.psum_scatter(grad_bias_qv, "dp", scatter_dimension=1, tiled=True),
        lax.psum_scatter(grad_out_w, "dp", scatter_dimension=1, tiled=True),
        lax.psum_scatter(grad_up_w, "dp", scatter_dimension=0, tiled=True),
        lax.psum_scatter(grad_bias_up, "dp", scatter_dimension=0, tiled=True),
        lax.psum_scatter(grad_down_w, "dp", scatter_dimension=1, tiled=True),
    )
    g_bout, g_bdown, g_gone, g_sone, g_gtwo, g_stwo = (
        lax.psum_scatter(d_bias_out, ("dp", "tensor"), scatter_dimension=0, tiled=True),
        lax.psum_scatter(d_bias_down, ("dp", "tensor"), scatter_dimension=0, tiled=True),
        lax.psum_scatter(d_gain_one, ("dp", "tensor"), scatter_dimension=0, tiled=True),
        lax.psum_scatter(d_shift_one, ("dp", "tensor"), scatter_dimension=0, tiled=True),
        lax.psum_scatter(d_gain_two, ("dp", "tensor"), scatter_dimension=0, tiled=True),
        lax.psum_scatter(d_shift_two, ("dp", "tensor"), scatter_dimension=0, tiled=True),
    )
    return (
        layer_out.astype(jnp.bfloat16),
        d_tokens.astype(jnp.bfloat16),
        g_qkv,
        g_bqv,
        g_out,
        g_up,
        g_bup,
        g_down,
        g_bout,
        g_bdown,
        g_gone,
        g_sone,
        g_gtwo,
        g_stwo,
    )


def solution(mesh):
    return jax.shard_map(
        local,
        mesh=mesh,
        in_specs=(
            P(("dp", "tensor"), None),
            P(("dp", "tensor"), None),
            P("dp", None),
            P(None, "dp", "tensor"),
            P(None, ("tensor", "dp")),
            P("tensor", "dp"),
            P("dp", "tensor"),
            P(("tensor", "dp")),
            P("tensor", "dp"),
            P(("dp", "tensor")),
            P(("dp", "tensor")),
            P(("dp", "tensor")),
            P(("dp", "tensor")),
            P(("dp", "tensor")),
            P(("dp", "tensor")),
        ),
        out_specs=(
            P(("dp", "tensor"), None),
            P(("dp", "tensor"), None),
            P(None, "dp", "tensor"),
            P(None, ("tensor", "dp")),
            P("tensor", "dp"),
            P("dp", "tensor"),
            P(("tensor", "dp")),
            P("tensor", "dp"),
            P(("dp", "tensor")),
            P(("dp", "tensor")),
            P(("dp", "tensor")),
            P(("dp", "tensor")),
            P(("dp", "tensor")),
            P(("dp", "tensor")),
        ),
        check_vma=False,
    )
```

profile of v0, /device:TPU:0, one launch (start us, length us, event | category | flops | bytes accessed | tf_op | source)
XLA Modules:
  0.0 854.5 jit_solution(17377182914923498748)
XLA Ops:
  8.8 22.3 %all-gather = bf16[8,24,2]{1,2,0:T(2,128)(2,1)S(1)} all-gather(bf16[1,24,2]{1,2,0:T(2,128)(2,1)} %bitcast.205), channel_id=1, replica_groups=mesh['dp'=8,'tensor'=4] {'dp'}, dimensions={0}, use_global_device_ids=true | all-gather | bytes 864 | tf_op jit(solution)/shard_map/all_gather | solution.py:87
  34.5 31.1 %all_gather.55 = bf16[192,768]{0,1:T(8,128)(2,1)S(1)} all-gather(bf16[192,96]{0,1:T(8,128)(2,1)S(1)} %copy.55), channel_id=1, replica_groups=mesh['dp'=8,'tensor'=4] {'dp'}, dimensions={1}, use_global_device_ids=true | all-gather | bytes 331776 | tf_op jit(solution)/shard_map/all_gather | solution.py:88
  65.6 35.3 %all_gather.52 = bf16[3,768,192]{2,0,1:T(4,128)(2,1)} all-gather(bf16[3,96,192]{2,0,1:T(4,128)(2,1)S(1)} %copy.49), channel_id=1, replica_groups=mesh['dp'=8,'tensor'=4] {'dp'}, dimensions={1}, use_global_device_ids=true | all-gather | bytes 995328 | tf_op jit(solution)/shard_map/all_gather | solution.py:86
  100.9 5.2 fusion.60
  106.1 2.9 reshape.228
  114.2 40.8 %while.26 = (s32[]{:T(128)}, bf16[4,512,3,64]{1,3,2,0:T(8,128)(2,1)}, f32[4,3,512,1]{2,1,3,0:T(4,128)}, bf16[3,2,1024,3,64]{2,4,3,1,0:T(8,128)(2,1)S(1)}, s32[4]...) while((s32[]{:T(128)}, ...), condition=%wide.region_3.4_spmd, body=%wide.region_0.3_spmd.sunk | while | flops 422148608 | bytes 25370816 | solution.py:116
  121.1 2.7 fusion.132
  131.3 2.7 fusion.132
  141.5 2.7 fusion.132
  151.7 2.7 fusion.132
  158.2 2.7 convolution_convert_fusion.2
  168.5 39.5 %all-reduce.16 = (f32[768]{0:T(1024)}, f32[768]{0:T(1024)}, f32[768]{0:T(1024)S(1)}, f32[768]{0:T(1024)}, f32[768]{0:T(1024)}) all-reduce(f32[768]{0:T(1024)} %dynamic-update-slice.2, f32[768]{0:T(1024)} %dynamic-update-slice.1, f32[768]{0:T(1024)} %dynamic-update-slice, ...), channel_id=1, replica_groups=mesh['dp'=8,'tensor'=4] {'dp','tensor'}, use_global_device_ids=true, to_apply=%add.2 | all-reduce | flops 3840 | bytes 30720
  218.3 21.6 %all-reduce.3 = bf16[768]{0:T(1024)(128)(2,1)} all-reduce(bf16[768]{0:T(1024)(128)(2,1)} %dynamic-update-slice.3), channel_id=1, replica_groups=mesh['dp'=8,'tensor'=4] {'dp'}, use_global_device_ids=true, to_apply=%add.3 | all-reduce | flops 768 | bytes 3072
  243.2 7.0 multiply_convert_fusion.1
  250.1 36.9 %all-gather.14.cloned.1.call-done = bf16[768,768]{0,1:T(8,128)(2,1)} async-done(((bf16[768,96]{0,1:T(8,128)(2,1)}), bf16[768,768]{0,1:T(8,128)(2,1)}) %all-gather.14.cloned.1.call-update) | async-done | bytes 1179664 | tf_op jit(solution)/shard_map/all_gather | solution.py:91
  287.0 6.5 convolution_convert_fusion.1
  293.6 36.3 %reduce-scatter.16.cloned.1.call-done = bf16[512,768]{1,0:T(8,128)(2,1)} async-done(((bf16[2048,768]{1,0:T(8,128)(2,1)}), bf16[512,768]{1,0:T(8,128)(2,1)}) %reduce-scatter.16.cloned.1.call-update) | async-done | bytes 786448 | tf_op jit(solution)/shard_map/reduce_scatter | solution.py:135
  337.4 28.6 %all-gather.16.cloned.1.call-done = bf16[2048,768]{1,0:T(8,128)(2,1)} async-done(((bf16[512,768]{1,0:T(8,128)(2,1)}), bf16[2048,768]{1,0:T(8,128)(2,1)}) %all-gather.16.cloned.1.call-update) | async-done | bytes 3145744 | tf_op jit(solution)/shard_map/all_gather | solution.py:155
  366.0 8.0 convert_reduce_fusion
  375.7 4.0 convolution_convert_fusion
  379.8 37.9 %reduce-scatter.18.cloned.1.call-done = bf16[512,768]{1,0:T(8,128)(2,1)} async-done(((bf16[2048,768]{1,0:T(8,128)(2,1)}), bf16[512,768]{1,0:T(8,128)(2,1)}) %reduce-scatter.18.cloned.1.call-update) | async-done | bytes 786448 | tf_op jit(solution)/shard_map/reduce_scatter | solution.py:163
  417.7 3.6 multiply_reduce_fusion.1
  426.3 28.4 %all-gather.18.cloned.1.call-done = bf16[2048,768]{1,0:T(8,128)(2,1)} async-done(((bf16[512,768]{1,0:T(8,128)(2,1)}), bf16[2048,768]{1,0:T(8,128)(2,1)}) %all-gather.18.cloned.1.call-update) | async-done | bytes 3145744 | tf_op jit(solution)/shard_map/all_gather | solution.py:170
  454.8 4.0 convolution_convert_fusion.3
  458.7 3.1 reshape.231
  463.9 61.6 %while.27 = (s32[]{:T(128)}, bf16[4,512,3,64]{1,3,2,0:T(8,128)(2,1)}, f32[4,1024,3,64]{1,3,2,0:T(8,128)}, f32[4,1024,3,64]{1,3,2,0:T(8,128)}, bf16[3,2,1024,3,64...) while((s32[]{:T(128)}, ...), condition=%wide.region_17.18_spmd, body=%wide.region_15.17_spmd.sunk | while | flops 1031043584 | bytes 65866036 | solution.py:181
  469.5 2.8 fusion.145
  485.0 2.8 fusion.145
  500.4 2.8 fusion.145
  503.1 2.5 multiply_reduce_fusion.6
  515.7 2.8 fusion.145
  525.6 4.4 convolution_bitcast_fusion
  531.5 4.6 bitcast_reduce_fusion
  537.8 2.5 stack_reshape.14
  540.4 2.8 copy.60
  543.2 3.2 stack_reshape.13
  547.7 6.0 fusion.67
  553.7 4.2 copy.64
  557.9 4.7 reshape.255
  562.7 5.6 bitcast_convert_fusion
  568.6 7.0 fusion.86
  575.7 6.9 fusion.87
  584.4 40.5 %all-reduce.15 = (f32[768]{0:T(1024)S(1)}, f32[768]{0:T(1024)S(1)}, f32[768]{0:T(1024)S(1)}, f32[768]{0:T(1024)S(1)}, f32[768]{0:T(1024)S(1)}, /*index=5*/f32[768]{0:T(1024)S(1)}, f32[768]{0:T(1024)S(1)}) all-reduce(f32[768]{0:T(1024)S(1)} %dynamic-update-slice.6, ...), channel_id=1, replica_groups=mesh['dp'=8,'tensor'=4] {'dp','tensor'}, use_global_device_ids=true, to_apply=%add.6 | all-reduce | flops 5376 | bytes 43008
  630.0 21.5 %all-reduce.17 = (f32[2,192]{1,0:T(2,128)S(1)}, f32[768]{0:T(1024)S(1)}) all-reduce(f32[2,192]{1,0:T(2,128)S(1)} %pad_maximum_fusion, f32[768]{0:T(1024)S(1)} %copy-done.40), channel_id=7, replica_groups=mesh['dp'=8,'tensor'=4] {'dp'}, use_global_device_ids=true, to_apply=%region_23.24.clone | all-reduce | flops 1152 | bytes 9216
  654.3 8.0 reduce-scatter.26.cloned.1.call-done
  664.2 37.5 %reduce-scatter.20.cloned.1.call-done = bf16[512,768]{1,0:T(8,128)(2,1)} async-done(((bf16[2048,768]{1,0:T(8,128)(2,1)}), bf16[512,768]{1,0:T(8,128)(2,1)}) %reduce-scatter.20.cloned.1.call-update) | async-done | bytes 786448 | tf_op jit(solution)/shard_map/reduce_scatter | solution.py:197
  704.0 70.6 %reduce-scatter.22.cloned.1.call-done = f32[96,768]{1,0:T(8,128)} async-done(((f32[768,768]{1,0:T(8,128)}), f32[96,768]{1,0:T(8,128)}) %reduce-scatter.22.cloned.1.call-update) | async-done | bytes 294928 | tf_op jit(solution)/shard_map/reduce_scatter | solution.py:209
  774.6 72.4 %reduce-scatter.24.cloned.1.call-done = f32[768,96]{0,1:T(8,128)} async-done(((f32[768,768]{0,1:T(8,128)}), f32[768,96]{0,1:T(8,128)}) %reduce-scatter.24.cloned.1.call-update) | async-done | bytes 294928 | tf_op jit(solution)/shard_map/reduce_scatter | solution.py:211
  (295 shorter events, 128.2 us)
Async XLA Ops:
  8.0 92.9 %all-gather.8.cloned.1.call-start = ((), (), s32[]{:S(2)}) async-start(), calls=%async_computation.8 | async-start | bytes 3932160 | tf_op jit(solution)/shard_map/all_gather | solution.py:103
  8.7 199.3 %reduce-scatter.14.cloned.1.call-start = ((), (), s32[]{:S(2)}) async-start(), calls=%async_computation.9 | async-start | bytes 3932160 | tf_op jit(solution)/shard_map/reduce_scatter | solution.py:120
  111.5 2.8 copy-start.20
  155.0 2.2 copy-start.7
  155.1 5.8 copy-start.21
  160.9 47.1 %copy-start.2 = (bf16[512,768]{1,0:T(8,128)(2,1)S(1)}, bf16[512,768]{1,0:T(8,128)(2,1)}, u32[]{:S(2)}) copy-start(bf16[512,768]{1,0:T(8,128)(2,1)} %param.19) | copy-start | bytes 2359300
  160.9 80.3 %all-gather.12.cloned.1.call-start = ((), (), s32[]{:S(2)}) async-start(), calls=%async_computation.11 | async-start | bytes 1327104 | tf_op jit(solution)/shard_map/all_gather | solution.py:89
  161.5 81.7 %all-gather.10.cloned.1.call-start = ((), (), s32[]{:S(2)}) async-start(), calls=%async_computation.10 | async-start | bytes 3932160 | tf_op jit(solution)/shard_map/all_gather | solution.py:130
  162.6 4.5 copy-start.36
  208.0 4.3 copy-start.3
  208.0 4.3 copy-start.22
  208.0 4.3 copy-start.37
  213.7 73.3 %all-gather.14.cloned.1.call-start = ((), (), s32[]{:S(2)}) async-start(), calls=%async_computation.12 | async-start | bytes 1327104 | tf_op jit(solution)/shard_map/all_gather | solution.py:91
  214.3 115.7 %reduce-scatter.16.cloned.1.call-start = ((), (), s32[]{:S(2)}) async-start(), calls=%async_computation.13 | async-start | bytes 3932160 | tf_op jit(solution)/shard_map/reduce_scatter | solution.py:135
  293.5 72.5 %all-gather.16.cloned.1.call-start = ((), (), s32[]{:S(2)}) async-start(), calls=%async_computation.14 | async-start | bytes 3932160 | tf_op jit(solution)/shard_map/all_gather | solution.py:155
  329.9 2.6 copy-start.14
  329.9 2.6 copy-start.27
  332.2 2.3 copy-start
  332.2 2.3 copy-start.25
  332.5 1.9 copy-start.30
  334.5 2.8 copy-start.29
  337.3 80.4 %reduce-scatter.18.cloned.1.call-start = ((), (), s32[]{:S(2)}) async-start(), calls=%async_computation.15 | async-start | bytes 3932160 | tf_op jit(solution)/shard_map/reduce_scatter | solution.py:163
  366.0 9.7 %copy-start.41 = (bf16[768,768]{1,0:T(8,128)(2,1)S(1)}, bf16[768,768]{1,0:T(8,128)(2,1)}, u32[]{:S(2)}) copy-start(bf16[768,768]{1,0:T(8,128)(2,1)} %all-gather.12.cloned.1.call-done) | copy-start | bytes 3538948
  379.7 75.0 %all-gather.18.cloned.1.call-start = ((), (), s32[]{:S(2)}) async-start(), calls=%async_computation.16 | async-start | bytes 3932160 | tf_op jit(solution)/shard_map/all_gather | solution.py:170
  417.7 4.3 copy-start.4
  417.7 4.3 copy-start.6
  417.7 4.3 copy-start.15
  417.7 4.3 copy-start.23
  426.1 226.6 %reduce-scatter.28.cloned.1.call-start = ((), (), s32[]{:S(2)}) async-start(), calls=%async_computation.21 | async-start | bytes 884736
  458.7 5.2 copy-start.8
  458.7 5.2 copy-start.44
  474.8 1.8 copy-start.17
  490.2 1.8 copy-start.17
  505.6 1.8 copy-start.17
  521.0 1.8 copy-start.17
  525.6 4.7 copy-start.19
  530.0 132.3 %reduce-scatter.26.cloned.1.call-start = ((), (), s32[]{:S(2)}) async-start(), calls=%async_computation.20 | async-start | bytes 2211840
  547.7 15.0 %copy-start.11 = (bf16[3,2048,192]{1,2,0:T(8,128)(2,1)}, bf16[3,2048,192]{1,2,0:T(8,128)(2,1)S(1)}, u32[]{:S(2)}) copy-start(bf16[3,2048,192]{1,2,0:T(8,128)(2,1)S(1)} %constant_dynamic-update-slice_fusion) | copy-start | bytes 7077892
  562.7 139.1 %reduce-scatter.20.cloned.1.call-start = ((), (), s32[]{:S(2)}) async-start(), calls=%async_computation.17 | async-start | bytes 3932160 | tf_op jit(solution)/shard_map/reduce_scatter | solution.py:197
  568.3 206.3 %reduce-scatter.22.cloned.1.call-start = ((), (), s32[]{:S(2)}) async-start(), calls=%async_computation.18 | async-start | bytes 2654208 | tf_op jit(solution)/shard_map/reduce_scatter | solution.py:209
  575.6 271.4 %reduce-scatter.24.cloned.1.call-start = ((), (), s32[]{:S(2)}) async-start(), calls=%async_computation.19 | async-start | bytes 2654208 | tf_op jit(solution)/shard_map/reduce_scatter | solution.py:211
  582.6 1.8 copy-start.38
  582.6 45.8 %copy-start.1 = (f32[512,768]{1,0:T(8,128)S(1)}, f32[512,768]{1,0:T(8,128)}, u32[]{:S(2)}) copy-start(f32[512,768]{1,0:T(8,128)} %copy-done) | copy-start | bytes 4718596
  582.6 45.7 %copy-start.26 = (f32[512]{0:T(512)S(1)}, f32[512]{0:T(512)}, u32[]{:S(2)}) copy-start(f32[512]{0:T(512)} %copy-done.25) | copy-start | bytes 6148
  582.6 45.7 %copy-start.28 = (f32[768]{0:T(1024)S(1)}, f32[768]{0:T(1024)}, u32[]{:S(2)}) copy-start(f32[768]{0:T(1024)} %get-tuple-element.275) | copy-start | bytes 9220
  582.7 45.7 %copy-start.31 = (f32[512]{0:T(512)S(1)}, f32[512]{0:T(512)}, u32[]{:S(2)}) copy-start(f32[512]{0:T(512)} %copy-done.30) | copy-start | bytes 6148
  624.9 4.7 copy-start.12
  629.6 72.1 %copy-start.10 = (f32[512,768]{1,0:T(8,128)S(1)}, f32[512,768]{1,0:T(8,128)}, u32[]{:S(2)}) copy-start(f32[512,768]{1,0:T(8,128)} %copy-done.9) | copy-start | bytes 4718596
  (21 other events, 28.0 us)
Sparse Core Ops, SparseCore 0:
  10.4 31.2 all-gather.7
  161.0 36.9 reduce-scatter.13
  337.5 28.5 all-gather.15
  426.2 28.5 all-gather.17
Sparse Core Ops, SparseCore 1:
  163.6 40.2 all-gather.11
  213.8 29.3 all-gather.9
  245.4 41.5 all-gather.13
  293.6 36.3 reduce-scatter.15
  379.8 37.8 reduce-scatter.17
  530.1 62.5 reduce-scatter.27
  596.0 66.3 reduce-scatter.25
  664.9 36.8 reduce-scatter.19
  705.7 68.9 reduce-scatter.21
  778.7 68.2 reduce-scatter.23
where the time goes:
time: 865 us; the launch traced here: 855 us
  waiting for transfers between devices  361 us (42%)
  blocking collectives  212 us (25%)
  matrix products  120 us (14%)
  local copies, waits for them, and re-layouts  79.5 us (9%)
  other arithmetic  47.5 us (5%)
  between operations  18.4 us (2%)
  loops' own time  16 us (2%)
    unnamed x4, blocking collectives  123 us
    reduce_scatter x1, waiting for transfers between devices, local(): lax.psum_scatter(grad_down_w, 'dp', scatter_dimension=1, tiled=True)  72.4 us
    reduce_scatter x1, waiting for transfers between devices, local(): lax.psum_scatter(grad_up_w, 'dp', scatter_dimension=0, tiled=True)  70.6 us
    reduce_scatter x1, waiting for transfers between devices, local(): lax.psum_scatter(contract_cols(part, wup_b).astype(jnp.bfloat16), 'tensor...  37.9 us
    reduce_scatter x1, waiting for transfers between devices, local(): lax.psum_scatter(jnp.einsum('jte,jde->td', part, wqkv_b, preferred_elemen...  37.5 us
    unnamed x120, local copies, waits for them, and re-layouts  37.3 us
    all_gather x1, waiting for transfers between devices, local(): lax.all_gather(w_down, 'dp', axis=1, tiled=True)  36.9 us
    reduce_scatter x1, waiting for transfers between devices, local(): lax.psum_scatter(jnp.dot(part, wdown_l, preferred_element_type=jnp.float3...  36.3 us
  transfers between devices with their start and end apart: 14, of which 10 were waited for; matrix products, arithmetic and copies ran while one was open for 11% of the time, Pallas kernels for 0%

commit v1 on v0

--- a/solution.py
+++ b/solution.py
@@ -152,7 +152,14 @@
     d_second, d_gain_two, d_shift_two = pull_two(grad_out.astype(jnp.float32))
     d_branch = d_second.astype(jnp.bfloat16)
     d_bias_down = jnp.sum(d_branch.astype(jnp.float32), axis=0)
-    branch_full = lax.all_gather(d_branch, "tensor", axis=0, tiled=True)
+    ring = [d_branch]
+    for hop in range(3):
+        ring.append(lax.ppermute(ring[-1], "tensor", [(dev, (dev + 1) % 4) for dev in range(4)]))
+    branch_full = jnp.roll(
+        jnp.concatenate(ring[::-1], axis=0),
+        (lax.axis_index("tensor") + 1) * ring[0].shape[0],
+        axis=0,
+    )
     grad_down_w = contract_rows(hidden, branch_full)
     d_hidden = contract_cols(branch_full, wdown_b)
     _, pull_gelu = jax.vjp(gelu_exact, up)

time: 865 us -> 880 us (1.017)
  local copies, waits for them, and re-layouts: 79.5 us -> 88.9 us
  starting transfers between devices: 1.23 us -> 10.6 us
    ppermute x0 -> x3, waiting for transfers between devices: none -> 34.6 us  [local(): lax.ppermute(ring[-1], 'tensor', [(dev, (dev + 1) % 4) for dev in range(4)])]
    all_gather x1 -> x0, waiting for transfers between devices: 28.6 us -> none  [local(): branch_full = lax.all_gather(d_branch, 'tensor', axis=0, tiled=True)]
    all_gather x1, starting transfers between devices: 0.04 us -> 9.57 us  [local(): attn_full = lax.all_gather(d_attn, 'tensor', axis=0, tiled=True)]
    reduce_scatter x1, waiting for transfers between devices: 37.9 us -> 28.5 us  [local(): lax.psum_scatter(contract_cols(part, wup_b).astype(jnp.bfloat16), 'tensor...]
    unnamed x120 -> x139, local copies, waits for them, and re-layouts: 37.3 us -> 44.1 us
  transfers between devices with their start and end apart: 14 -> 16, of which waited for: 10 -> 12; matrix products, arithmetic and copies ran while one was open for 11% -> 10% of each run, Pallas kernels for 0% -> 0%
where the time goes in v1:
time: 880 us; the launch traced here: 869 us
  waiting for transfers between devices  357 us (41%)
  blocking collectives  211 us (24%)
  matrix products  121 us (14%)
  local copies, waits for them, and re-layouts  88.9 us (10%)
  other arithmetic  46.5 us (5%)
  between operations  18.5 us (2%)
  loops' own time  16 us (2%)
  starting transfers between devices  10.6 us (1%)
    unnamed x4, blocking collectives  123 us
    reduce_scatter x1, waiting for transfers between devices, local(): lax.psum_scatter(grad_down_w, 'dp', scatter_dimension=1, tiled=True)  72.3 us
    reduce_scatter x1, waiting for transfers between devices, local(): lax.psum_scatter(grad_up_w, 'dp', scatter_dimension=0, tiled=True)  70.6 us
    unnamed x139, local copies, waits for them, and re-layouts  44.1 us
    reduce_scatter x1, waiting for transfers between devices, local(): lax.psum_scatter(jnp.einsum('jte,jde->td', part, wqkv_b, preferred_elemen...  37.5 us
    all_gather x1, waiting for transfers between devices, local(): lax.all_gather(w_down, 'dp', axis=1, tiled=True)  36.9 us
    reduce_scatter x1, waiting for transfers between devices, local(): lax.psum_scatter(jnp.dot(part, wdown_l, preferred_element_type=jnp.float3...  36.3 us
    all_gather x1, blocking collectives, local(): lax.all_gather(w_qkv, 'dp', axis=1, tiled=True)  35.3 us
  transfers between devices with their start and end apart: 16, of which 12 were waited for; matrix products, arithmetic and copies ran while one was open for 10% of the time, Pallas kernels for 0%

profile of v1, /device:TPU:0, one launch (start us, length us, event | category | flops | bytes accessed | tf_op | source)
XLA Modules:
  0.0 869.4 jit_solution(6023441578728153)
XLA Ops:
  8.8 22.3 %all-gather = bf16[8,24,2]{1,2,0:T(2,128)(2,1)S(1)} all-gather(bf16[1,24,2]{1,2,0:T(2,128)(2,1)} %bitcast.203), channel_id=1, replica_groups=mesh['dp'=8,'tensor'=4] {'dp'}, dimensions={0}, use_global_device_ids=true | all-gather | bytes 864 | tf_op jit(solution)/shard_map/all_gather | solution.py:87
  34.5 31.1 %all_gather.52 = bf16[192,768]{0,1:T(8,128)(2,1)S(1)} all-gather(bf16[192,96]{0,1:T(8,128)(2,1)S(1)} %copy.55), channel_id=1, replica_groups=mesh['dp'=8,'tensor'=4] {'dp'}, dimensions={1}, use_global_device_ids=true | all-gather | bytes 331776 | tf_op jit(solution)/shard_map/all_gather | solution.py:88
  65.6 35.3 %all_gather.49 = bf16[3,768,192]{2,0,1:T(4,128)(2,1)} all-gather(bf16[3,96,192]{2,0,1:T(4,128)(2,1)S(1)} %copy.49), channel_id=1, replica_groups=mesh['dp'=8,'tensor'=4] {'dp'}, dimensions={1}, use_global_device_ids=true | all-gather | bytes 995328 | tf_op jit(solution)/shard_map/all_gather | solution.py:86
  100.9 5.2 fusion.60
  106.1 3.0 reshape.228
  114.3 40.8 %while.26 = (s32[]{:T(128)}, bf16[4,512,3,64]{1,3,2,0:T(8,128)(2,1)}, f32[4,3,512,1]{2,1,3,0:T(4,128)}, bf16[3,2,1024,3,64]{2,4,3,1,0:T(8,128)(2,1)S(1)}, s32[4]...) while((s32[]{:T(128)}, ...), condition=%wide.region_3.4_spmd, body=%wide.region_0.3_spmd.sunk | while | flops 422148608 | bytes 25370816 | solution.py:116
  121.1 2.7 fusion.137
  131.3 2.7 fusion.137
  141.5 2.7 fusion.137
  151.7 2.7 fusion.137
  168.6 39.4 %all-reduce.16 = (f32[768]{0:T(1024)}, f32[768]{0:T(1024)}, f32[768]{0:T(1024)S(1)}, f32[768]{0:T(1024)}, f32[768]{0:T(1024)}) all-reduce(f32[768]{0:T(1024)} %dynamic-update-slice.2, f32[768]{0:T(1024)} %dynamic-update-slice.1, f32[768]{0:T(1024)} %dynamic-update-slice, ...), channel_id=1, replica_groups=mesh['dp'=8,'tensor'=4] {'dp','tensor'}, use_global_device_ids=true, to_apply=%add.2 | all-reduce | flops 3840 | bytes 30720
  218.2 21.6 %all-reduce.3 = bf16[768]{0:T(1024)(128)(2,1)} all-reduce(bf16[768]{0:T(1024)(128)(2,1)} %dynamic-update-slice.3), channel_id=1, replica_groups=mesh['dp'=8,'tensor'=4] {'dp'}, use_global_device_ids=true, to_apply=%add.3 | all-reduce | flops 768 | bytes 3072
  243.1 7.0 multiply_convert_fusion.1
  250.1 36.9 %all-gather.13.cloned.1.call-done = bf16[768,768]{0,1:T(8,128)(2,1)} async-done(((bf16[768,96]{0,1:T(8,128)(2,1)}), bf16[768,768]{0,1:T(8,128)(2,1)}) %all-gather.13.cloned.1.call-update) | async-done | bytes 1179664 | tf_op jit(solution)/shard_map/all_gather | solution.py:91
  287.0 6.5 convolution_convert_fusion.1
  293.6 36.3 %reduce-scatter.16.cloned.1.call-done = bf16[512,768]{1,0:T(8,128)(2,1)} async-done(((bf16[2048,768]{1,0:T(8,128)(2,1)}), bf16[512,768]{1,0:T(8,128)(2,1)}) %reduce-scatter.16.cloned.1.call-update) | async-done | bytes 786448 | tf_op jit(solution)/shard_map/reduce_scatter | solution.py:135
  337.3 11.4 %collective-permute-done = bf16[512,768]{1,0:T(8,128)(2,1)S(1)} collective-permute-done((bf16[512,768]{1,0:T(8,128)(2,1)S(1)}, bf16[512,768]{1,0:T(8,128)(2,1)S(1)}, u32[]{:S(2)}, u32[]{:S(2)}) %collective-permute-start) | collective-permute-done | bytes 786464 | tf_op jit(solution)/shard_map/ppermute | solution.py:157
  349.6 11.5 %collective-permute-done.1 = bf16[512,768]{1,0:T(8,128)(2,1)} collective-permute-done((bf16[512,768]{1,0:T(8,128)(2,1)S(1)}, bf16[512,768]{1,0:T(8,128)(2,1)}, u32[]{:S(2)}, u32[]{:S(2)}) %collective-permute-start.1) | collective-permute-done | bytes 786464 | tf_op jit(solution)/shard_map/ppermute | solution.py:157
  361.1 11.7 %collective-permute-done.2 = bf16[512,768]{1,0:T(8,128)(2,1)} collective-permute-done((bf16[512,768]{1,0:T(8,128)(2,1)}, bf16[512,768]{1,0:T(8,128)(2,1)}, u32[]{:S(2)}, u32[]{:S(2)}) %collective-permute-start.2) | collective-permute-done | bytes 786464 | tf_op jit(solution)/shard_map/ppermute | solution.py:157
  378.0 8.7 %convert_reduce_fusion = (f32[768]{0:T(1024)}, bf16[2048,768]{1,0:T(8,128)(2,1)S(1)}) fusion(bf16[768,768]{0,1:T(8,128)(2,1)S(1)} %copy-done.48, bf16[4096,768]{1,0:T(8,128)(2,1)S(1)} %constant_dynamic-update-slice_fusion, s32[]{:T(128)S(6)} %select_n.39, f32[2048,768]{1,0:T(8,128)} %get-tuple-element.303, f32[768]{0:T(1024)S(1)} %copy-done.46), kind=kOutput, calls=%fused_computation.66 | convolution fusion | flops 2441084160 | bytes 13769732 | tf_op jit(solution)/shard_map/dot_general | solution.py:58
  388.4 4.0 convolution_convert_fusion
  392.5 9.6 %all-gather.15.cloned.1.call-start = ((), (), s32[]{:S(2)}) async-start(), calls=%async_computation.15 | async-start | bytes 3932160 | tf_op jit(solution)/shard_map/all_gather | solution.py:177
  402.1 28.5 %reduce-scatter.18.cloned.1.call-done = bf16[512,768]{1,0:T(8,128)(2,1)} async-done(((bf16[2048,768]{1,0:T(8,128)(2,1)}), bf16[512,768]{1,0:T(8,128)(2,1)}) %reduce-scatter.18.cloned.1.call-update) | async-done | bytes 786448 | tf_op jit(solution)/shard_map/reduce_scatter | solution.py:170
  430.6 3.6 multiply_reduce_fusion.1
  439.0 28.4 %all-gather.15.cloned.1.call-done = bf16[2048,768]{1,0:T(8,128)(2,1)} async-done(((bf16[512,768]{1,0:T(8,128)(2,1)}), bf16[2048,768]{1,0:T(8,128)(2,1)}) %all-gather.15.cloned.1.call-update) | async-done | bytes 3145744 | tf_op jit(solution)/shard_map/all_gather | solution.py:177
  467.3 4.0 convolution_convert_fusion.3
  471.3 3.0 reshape.231
  476.4 64.3 %while.27 = (s32[]{:T(128)}, bf16[4,512,3,64]{1,3,2,0:T(8,128)(2,1)}, f32[4,1024,3,64]{1,3,2,0:T(8,128)}, f32[4,1024,3,64]{1,3,2,0:T(8,128)}, bf16[3,2,1024,3,64...) while((s32[]{:T(128)}, ...), condition=%wide.region_17.18_spmd, body=%wide.region_15.17_spmd.sunk | while | flops 1031043584 | bytes 65866036 | solution.py:188
  482.7 2.9 fusion.150
  498.9 2.8 fusion.150
  514.9 2.8 fusion.150
  530.9 2.8 fusion.150
  540.8 4.4 convolution_bitcast_fusion
  546.7 4.6 bitcast_reduce_fusion
  555.6 2.8 copy.60
  558.5 3.2 stack_reshape.13
  563.0 6.1 fusion.73
  569.0 4.3 copy.64
  573.3 4.7 reshape.255
  578.1 5.6 bitcast_convert_fusion
  584.0 6.9 fusion.94
  591.1 7.0 fusion.63
  599.8 40.5 %all-reduce.15 = (f32[768]{0:T(1024)S(1)}, f32[768]{0:T(1024)S(1)}, f32[768]{0:T(1024)S(1)}, f32[768]{0:T(1024)S(1)}, f32[768]{0:T(1024)S(1)}, /*index=5*/f32[768]{0:T(1024)S(1)}, f32[768]{0:T(1024)S(1)}) all-reduce(f32[768]{0:T(1024)S(1)} %dynamic-update-slice.6, ...), channel_id=1, replica_groups=mesh['dp'=8,'tensor'=4] {'dp','tensor'}, use_global_device_ids=true, to_apply=%add.6 | all-reduce | flops 5376 | bytes 43008
  645.4 21.3 %all-reduce.17 = (f32[2,192]{1,0:T(2,128)S(1)}, f32[768]{0:T(1024)S(1)}) all-reduce(f32[2,192]{1,0:T(2,128)S(1)} %pad_maximum_fusion, f32[768]{0:T(1024)S(1)} %copy-done.45), channel_id=7, replica_groups=mesh['dp'=8,'tensor'=4] {'dp'}, use_global_device_ids=true, to_apply=%region_23.24.clone | all-reduce | flops 1152 | bytes 9216
  669.6 7.7 reduce-scatter.26.cloned.1.call-done
  679.2 37.5 %reduce-scatter.20.cloned.1.call-done = bf16[512,768]{1,0:T(8,128)(2,1)} async-done(((bf16[2048,768]{1,0:T(8,128)(2,1)}), bf16[512,768]{1,0:T(8,128)(2,1)}) %reduce-scatter.20.cloned.1.call-update) | async-done | bytes 786448 | tf_op jit(solution)/shard_map/reduce_scatter | solution.py:204
  718.9 70.6 %reduce-scatter.22.cloned.1.call-done = f32[96,768]{1,0:T(8,128)} async-done(((f32[768,768]{1,0:T(8,128)}), f32[96,768]{1,0:T(8,128)}) %reduce-scatter.22.cloned.1.call-update) | async-done | bytes 294928 | tf_op jit(solution)/shard_map/reduce_scatter | solution.py:216
  789.6 72.3 %reduce-scatter.24.cloned.1.call-done = f32[768,96]{0,1:T(8,128)} async-done(((f32[768,768]{0,1:T(8,128)}), f32[768,96]{0,1:T(8,128)}) %reduce-scatter.24.cloned.1.call-update) | async-done | bytes 294928 | tf_op jit(solution)/shard_map/reduce_scatter | solution.py:218
  (318 shorter events, 144.3 us)
Async XLA Ops:
  8.0 92.9 %all-gather.7.cloned.1.call-start = ((), (), s32[]{:S(2)}) async-start(), calls=%async_computation.8 | async-start | bytes 3932160 | tf_op jit(solution)/shard_map/all_gather | solution.py:103
  8.7 199.2 %reduce-scatter.14.cloned.1.call-start = ((), (), s32[]{:S(2)}) async-start(), calls=%async_computation.9 | async-start | bytes 3932160 | tf_op jit(solution)/shard_map/reduce_scatter | solution.py:120
  109.1 5.2 copy-start.24
  155.1 5.9 copy-start.25
  158.2 49.8 %copy-start.2 = (bf16[512,768]{1,0:T(8,128)(2,1)S(1)}, bf16[512,768]{1,0:T(8,128)(2,1)}, u32[]{:S(2)}) copy-start(bf16[512,768]{1,0:T(8,128)(2,1)} %param.19) | copy-start | bytes 2359300
  161.0 80.1 %all-gather.11.cloned.1.call-start = ((), (), s32[]{:S(2)}) async-start(), calls=%async_computation.11 | async-start | bytes 1327104 | tf_op jit(solution)/shard_map/all_gather | solution.py:89
  161.5 81.6 %all-gather.9.cloned.1.call-start = ((), (), s32[]{:S(2)}) async-start(), calls=%async_computation.10 | async-start | bytes 3932160 | tf_op jit(solution)/shard_map/all_gather | solution.py:130
  162.7 4.5 copy-start.41
  208.0 4.3 copy-start.3
  208.0 4.3 copy-start.27
  208.0 4.3 copy-start.42
  213.6 73.3 %all-gather.13.cloned.1.call-start = ((), (), s32[]{:S(2)}) async-start(), calls=%async_computation.12 | async-start | bytes 1327104 | tf_op jit(solution)/shard_map/all_gather | solution.py:91
  214.2 115.7 %reduce-scatter.16.cloned.1.call-start = ((), (), s32[]{:S(2)}) async-start(), calls=%async_computation.13 | async-start | bytes 3932160 | tf_op jit(solution)/shard_map/reduce_scatter | solution.py:135
  293.5 137.1 %reduce-scatter.18.cloned.1.call-start = ((), (), s32[]{:S(2)}) async-start(), calls=%async_computation.14 | async-start | bytes 3932160 | tf_op jit(solution)/shard_map/reduce_scatter | solution.py:170
  334.4 26.6 %copy-start.34 = (f32[512]{0:T(512)}, f32[512]{0:T(512)S(1)}, u32[]{:S(2)}) copy-start(f32[512]{0:T(512)S(1)} %negate_multiply_fusion.1) | copy-start | bytes 6148
  337.3 11.4 %collective-permute-start = (bf16[512,768]{1,0:T(8,128)(2,1)S(1)}, bf16[512,768]{1,0:T(8,128)(2,1)S(1)}, u32[]{:S(2)}, u32[]{:S(2)}) collective-permute-start(bf16[512,768]{1,0:T(8,128)(2,1)S(1)} %get-tuple-element.279), channel_id=1, source_target_pairs={{0,1},{1,2},{2,3},{3,0},{4,5},{5,6},{6,7},{7,4},{8,9},{9,10},{10,1... | collective-permute-start | bytes 2359304 | tf_op jit(solution)/shard_map/ppermute | solution.py:157
  349.6 11.5 %collective-permute-start.1 = (bf16[512,768]{1,0:T(8,128)(2,1)S(1)}, bf16[512,768]{1,0:T(8,128)(2,1)}, u32[]{:S(2)}, u32[]{:S(2)}) collective-permute-start(bf16[512,768]{1,0:T(8,128)(2,1)S(1)} %collective-permute-done), channel_id=1, source_target_pairs={{0,1},{1,2},{2,3},{3,0},{4,5},{5,6},{6,7},{7,4},{8,9},{9,10},{10,1... | collective-permute-start | bytes 2359304 | tf_op jit(solution)/shard_map/ppermute | solution.py:157
  361.1 11.7 %collective-permute-start.2 = (bf16[512,768]{1,0:T(8,128)(2,1)}, bf16[512,768]{1,0:T(8,128)(2,1)}, u32[]{:S(2)}, u32[]{:S(2)}) collective-permute-start(bf16[512,768]{1,0:T(8,128)(2,1)} %collective-permute-done.1), channel_id=1, source_target_pairs={{0,1},{1,2},{2,3},{3,0},{4,5},{5,6},{6,7},{7,4},{8,9},{9,10},{10,1... | collective-permute-start | bytes 2359304 | tf_op jit(solution)/shard_map/ppermute | solution.py:157
  361.1 14.1 %copy-start.17 = (bf16[512,768]{1,0:T(8,128)(2,1)S(1)}, bf16[512,768]{1,0:T(8,128)(2,1)}, u32[]{:S(2)}) copy-start(bf16[512,768]{1,0:T(8,128)(2,1)} %copy-done.16) | copy-start | bytes 2359300
  361.1 14.2 %copy-start.12 = (bf16[512,768]{1,0:T(8,128)(2,1)S(1)}, bf16[512,768]{1,0:T(8,128)(2,1)}, u32[]{:S(2)}) copy-start(bf16[512,768]{1,0:T(8,128)(2,1)} %copy-done.11) | copy-start | bytes 2359300
  378.0 8.8 %copy-start.26 = (bf16[4096,768]{1,0:T(8,128)(2,1)}, bf16[4096,768]{1,0:T(8,128)(2,1)S(1)}, u32[]{:S(2)}) copy-start(bf16[4096,768]{1,0:T(8,128)(2,1)S(1)} %constant_dynamic-update-slice_fusion) | copy-start | bytes 18874372
  378.0 10.5 %copy-start.47 = (bf16[768,768]{1,0:T(8,128)(2,1)S(1)}, bf16[768,768]{1,0:T(8,128)(2,1)}, u32[]{:S(2)}) copy-start(bf16[768,768]{1,0:T(8,128)(2,1)} %all-gather.11.cloned.1.call-done) | copy-start | bytes 3538948
  392.5 74.8 %all-gather.15.cloned.1.call-start = ((), (), s32[]{:S(2)}) async-start(), calls=%async_computation.15 | async-start | bytes 3932160 | tf_op jit(solution)/shard_map/all_gather | solution.py:177
  430.6 4.2 copy-start.4
  430.6 4.2 copy-start.6
  430.6 4.2 copy-start.19
  430.6 4.2 copy-start.28
  438.9 229.1 %reduce-scatter.28.cloned.1.call-start = ((), (), s32[]{:S(2)}) async-start(), calls=%async_computation.20 | async-start | bytes 884736
  438.9 37.5 %copy-start.8 = (bf16[4,512,3,64]{1,3,2,0:T(8,128)(2,1)S(1)}, bf16[4,512,3,64]{1,3,2,0:T(8,128)(2,1)}, u32[]{:S(2)}) copy-start(bf16[4,512,3,64]{1,3,2,0:T(8,128)(2,1)} %copy-done.7) | copy-start | bytes 2359300
  540.8 4.7 copy-start.23
  545.3 132.0 %reduce-scatter.26.cloned.1.call-start = ((), (), s32[]{:S(2)}) async-start(), calls=%async_computation.19 | async-start | bytes 2211840
  563.0 15.1 %copy-start.13 = (bf16[3,2048,192]{1,2,0:T(8,128)(2,1)}, bf16[3,2048,192]{1,2,0:T(8,128)(2,1)S(1)}, u32[]{:S(2)}) copy-start(bf16[3,2048,192]{1,2,0:T(8,128)(2,1)S(1)} %constant_dynamic-update-slice_fusion.8) | copy-start | bytes 7077892
  578.0 138.7 %reduce-scatter.20.cloned.1.call-start = ((), (), s32[]{:S(2)}) async-start(), calls=%async_computation.16 | async-start | bytes 3932160 | tf_op jit(solution)/shard_map/reduce_scatter | solution.py:204
  583.7 205.9 %reduce-scatter.22.cloned.1.call-start = ((), (), s32[]{:S(2)}) async-start(), calls=%async_computation.17 | async-start | bytes 2654208 | tf_op jit(solution)/shard_map/reduce_scatter | solution.py:216
  590.9 8.6 copy-start.50
  590.9 8.8 %copy-start.38 = (f32[768]{0:T(1024)S(1)}, f32[768]{0:T(1024)}, u32[]{:S(2)}) copy-start(f32[768]{0:T(1024)} %get-tuple-element.222) | copy-start | bytes 9220
  590.9 8.8 %copy-start.39 = (f32[768]{0:T(1024)S(1)}, f32[768]{0:T(1024)}, u32[]{:S(2)}) copy-start(f32[768]{0:T(1024)} %get-tuple-element.225) | copy-start | bytes 9220
  590.9 8.8 %copy-start.40 = (f32[768]{0:T(1024)S(1)}, f32[768]{0:T(1024)}, u32[]{:S(2)}) copy-start(f32[768]{0:T(1024)} %get-tuple-element.278) | copy-start | bytes 9220
  591.0 8.8 %copy-start.43 = (f32[768]{0:T(1024)S(1)}, f32[768]{0:T(1024)}, u32[]{:S(2)}) copy-start(f32[768]{0:T(1024)} %get-tuple-element.220) | copy-start | bytes 9220
  591.0 8.8 %copy-start.44 = (f32[768]{0:T(1024)S(1)}, f32[768]{0:T(1024)}, u32[]{:S(2)}) copy-start(f32[768]{0:T(1024)} %get-tuple-element.224) | copy-start | bytes 9220
  591.0 52.8 %copy-start.31 = (f32[512]{0:T(512)S(1)}, f32[512]{0:T(512)}, u32[]{:S(2)}) copy-start(f32[512]{0:T(512)} %copy-done.30) | copy-start | bytes 6148
  591.0 52.8 %copy-start.33 = (f32[768]{0:T(1024)S(1)}, f32[768]{0:T(1024)}, u32[]{:S(2)}) copy-start(f32[768]{0:T(1024)} %get-tuple-element.275) | copy-start | bytes 9220
  591.0 52.8 %copy-start.36 = (f32[512]{0:T(512)S(1)}, f32[512]{0:T(512)}, u32[]{:S(2)}) copy-start(f32[512]{0:T(512)} %copy-done.35) | copy-start | bytes 6148
  591.0 270.8 %reduce-scatter.24.cloned.1.call-start = ((), (), s32[]{:S(2)}) async-start(), calls=%async_computation.18 | async-start | bytes 2654208 | tf_op jit(solution)/shard_map/reduce_scatter | solution.py:218
  598.0 45.7 %copy-start.1 = (f32[512,768]{1,0:T(8,128)S(1)}, f32[512,768]{1,0:T(8,128)}, u32[]{:S(2)}) copy-start(f32[512,768]{1,0:T(8,128)} %copy-done) | copy-start | bytes 4718596
  598.0 47.3 %copy-start.45 = (f32[768]{0:T(1024)S(1)}, f32[768]{0:T(1024)}, u32[]{:S(2)}) copy-start(f32[768]{0:T(1024)} %get-tuple-element.304) | copy-start | bytes 9220
  640.2 4.7 copy-start.14
  645.0 71.7 %copy-start.10 = (f32[512,768]{1,0:T(8,128)S(1)}, f32[512,768]{1,0:T(8,128)}, u32[]{:S(2)}) copy-start(f32[512,768]{1,0:T(8,128)} %copy-done.9) | copy-start | bytes 4718596
  (29 other events, 45.9 us)
Sparse Core Ops, SparseCore 0:
  10.4 31.2 all-gather.6
  161.1 36.9 reduce-scatter.13
  392.6 37.9 reduce-scatter.17
Sparse Core Ops, SparseCore 1:
  163.6 40.1 all-gather.10
  213.7 29.3 all-gather.8
  245.4 41.5 all-gather.12
  293.6 36.3 reduce-scatter.15
  438.9 28.3 all-gather.14
  545.3 62.5 reduce-scatter.27
  611.2 66.0 reduce-scatter.25
  679.9 36.8 reduce-scatter.19
  720.6 68.9 reduce-scatter.21
  793.6 68.1 reduce-scatter.23
